TPU v7x, 32 devices: a whole 2x2x4 slice. The times are simulated.
32 devices in a mesh: row: 16 (over z, y, x), col: 2 (over core).
Axes of the slice: x: 2, y: 2, z: 4, core: 2. Of those that a mesh axis runs over, the one named last changes fastest.
Arguments:
- vectors_in: bfloat16 [32768, 2048], P('row', 'col'), may hold values from -6 to 6
- panel: bfloat16 [32768, 256], P('row', 'col'), may hold values from -0.03125 to 0.03125
- factor: float32 [256, 256], replicated, may hold values from -3 to 8, as said below
- atom_basis: int32 [16, 128], P('row'), may hold values from 1 to 24, 2048 in all within a row
- proj_count: int32 [2048], P('row'), may hold values from 1 to 16
- coupling: bfloat16 [2048, 9, 384], P('row'), may hold values from -0.4375 to 0.4375
- block_present: int32 [2048, 9], P('row'), may hold values 0 or 1
- occ_mask: int32 [2048], P('col'), may hold values 0 or 1
- occ_weight: float32 [2048], P('col'), may hold values from 0.5 to 2
Outputs:
- vectors: bfloat16 [32768, 2048], P('row', 'col')
- density: float32 [2048, 256], P(('row', 'col'))
Inputs may be any that keep to these rules, and one draw needn't show every extreme that they name: `factor`: zero below the diagonal; the diagonal lies in 4 to 8. `atom_basis`: each row sums to 2048, and 24 is reached in each row.
All inputs are finite; a program needn't handle non-finite values. No bound on the sum of `block_present` or of `occ_mask` on one device may be relied on, other than what follows from the above.
Results may differ from a plain program's by a relative error of at most 0.0075.
Values may be sent and summed in bfloat16 or wider, within the bound.
A program may use at most 192 MiB of HBM per device.

v0:
```python
import jax
import jax.numpy as jnp
from jax import lax
from jax.sharding import PartitionSpec as P

NPMAX = 16
BMAX = 24
K = 9


def with_halo(array, sides, width):
    for axis, dim in sides:
        devices, length = (lax.axis_size(axis), array.shape[dim])
        up = [(i, (i + 1) % devices) for i in range(devices)]
        down = [(j, i) for i, j in up]
        last = lax.slice_in_dim(array, length - width, length, axis=dim)
        first = lax.slice_in_dim(array, 0, width, axis=dim)
        before = lax.ppermute(last, axis, up)
        after = lax.ppermute(first, axis, down)
        array = jnp.concatenate([before, array, after], axis=dim)
    return array


def panel_product(fragment, columns):
    return lax.dot_general(
        fragment, columns, (((0,), (0,)), ((), ())), preferred_element_type=jnp.float32
    )


def local(
    vectors_in, panel, factor, atom_basis, proj_count, coupling, block_present, occ_mask, occ_weight
):
    rows_here = vectors_in.shape[0]
    cols_here = vectors_in.shape[1]
    whole_panel = lax.all_gather(panel, "col", axis=1, tiled=True)
    inner_products = panel_product(whole_panel, vectors_in)
    inner_products = lax.psum(inner_products, "row")
    mixing = jnp.dot(factor.T, inner_products, precision=lax.Precision.HIGHEST).astype(jnp.bfloat16)
    update = jnp.dot(whole_panel, mixing, preferred_element_type=jnp.float32)
    vectors = (vectors_in.astype(jnp.float32) - update).astype(jnp.bfloat16)
    counts = atom_basis[0]
    atoms_here = counts.shape[0]
    starts = jnp.cumsum(counts) - counts
    slot_rank = jnp.arange(BMAX, dtype=jnp.int32)
    row_index = jnp.where(
        slot_rank[None, :] < counts[:, None], starts[:, None] + slot_rank[None, :], rows_here
    )
    padded = jnp.take(vectors, row_index.reshape(-1), axis=0, mode="fill", fill_value=0).reshape(
        atoms_here, BMAX, cols_here
    )
    rim_width = (K - 1) // 2
    extended = with_halo(padded, (("row", 0),), rim_width)
    projections = jnp.zeros((atoms_here, NPMAX, cols_here), jnp.float32)
    for relative in range(K):
        blocks = coupling[:, relative].reshape(atoms_here, NPMAX, BMAX)
        blocks = jnp.where(
            block_present[:, relative, None, None] > 0, blocks, jnp.zeros_like(blocks)
        )
        neighbours = extended[relative : relative + atoms_here]
        projections = projections + jnp.einsum(
            "aij,ajn->ain", blocks, neighbours, preferred_element_type=jnp.float32
        )
    kept_rows = (jnp.arange(NPMAX, dtype=jnp.int32)[None, :] < proj_count[:, None]).astype(
        jnp.float32
    )
    rounded = (projections * kept_rows[:, :, None]).astype(jnp.bfloat16)
    column_total = cols_here * lax.axis_size("col")
    weights = occ_mask.astype(jnp.float32) * occ_weight / column_total
    weighted = (rounded * weights[None, None, :]).astype(jnp.bfloat16)
    partial_value = jnp.einsum(
        "ain,ajn->aij", weighted, rounded, preferred_element_type=jnp.float32
    )
    partial_value = partial_value.reshape(atoms_here, NPMAX * NPMAX)
    density = lax.psum_scatter(
        partial_value.astype(jnp.bfloat16), "col", scatter_dimension=0, tiled=True
    ).astype(jnp.float32)
    return (vectors, density)


def solution(mesh):
    placed = (
        P("row", "col"),
        P("row", "col"),
        P(),
        P("row", None),
        P("row"),
        P("row", None, None),
        P("row", None),
        P("col"),
        P("col"),
    )
    return jax.shard_map(
        local,
        mesh=mesh,
        in_specs=placed,
        out_specs=(P("row", "col"), P(("row", "col"), None)),
        check_vma=False,
    )
```

profile of v0, /device:TPU:0, one launch (start us, length us, event | category | flops | bytes accessed | tf_op | source)
XLA Modules:
  0.0 292.0 jit_solution(12120854242485173018)
XLA Ops:
  7.2 0.7 all-gather.2.cloned.1.call-update
  8.0 0.8 copy.41
  8.7 0.2 reduce-window.8
  9.0 0.7 bitcast_subtract_fusion.1
  9.7 0.8 add_select_fusion
  10.6 1.4 fusion.48
  12.0 0.1 copy.67
  12.1 0.1 copy.68
  12.2 1.0 compare_bitcast_fusion.7
  13.3 0.4 copy.47
  13.7 6.5 %copy.39 = bf16[2048,1024]{0,1:T(8,128)(2,1)} copy(bf16[2048,1024]{1,0:T(8,128)(2,1)} %param.9) | data formatting | bytes 8388608 | tf_op args[0]
  20.3 0.1 copy.66
  20.5 1.2 copy.43
  21.7 1.2 copy.45
  22.9 0.4 copy.49
  23.3 0.1 copy.70
  23.5 0.1 copy.71
  23.6 1.2 copy.53
  24.8 1.2 copy.55
  26.1 0.1 copy.73
  26.3 1.2 copy.57
  27.5 0.4 copy.59
  28.1 0.4 copy.51
  28.7 4.8 %fusion.51 = f32[256,1024]{1,0:T(8,128)} fusion(bf16[2048,256]{1,0:T(8,128)(2,1)} %all-gather.2.cloned.1.call-done, bf16[2048,1024]{1,0:T(8,128)(2,1)} %param.9), kind=kOutput, calls=%fused_computation.88 | convolution fusion | flops 1073741824 | bytes 6291456 | tf_op jit(solution)/shard_map/dot_general | solution.py:25
  33.8 115.1 %all-reduce.2.cloned.1.call-done = f32[256,1024]{1,0:T(8,128)} async-done(((f32[256,1024]{1,0:T(8,128)}), f32[256,1024]{1,0:T(8,128)}) %all-reduce.2.cloned.1.call-update) | async-done | bytes 1048592 | tf_op jit(solution)/shard_map/psum | solution.py:37
  148.9 3.0 %convolution_convert_fusion = bf16[1024,256]{1,0:T(8,128)(2,1)S(1)} fusion(f32[256,1024]{1,0:T(8,128)} %all-reduce.2.cloned.1.call-done, f32[256,256]{1,0:T(8,128)S(1)} %copy-done), kind=kOutput, calls=%fused_computation.45 | convolution fusion | flops 805568512 | bytes 1835008 | tf_op jit(solution)/shard_map/dot_general | solution.py:38
  152.0 5.4 %fusion = bf16[2048,1024]{0,1:T(8,128)(2,1)} fusion(bf16[2048,1024]{0,1:T(8,128)(2,1)} %copy.39, bf16[1024,256]{1,0:T(8,128)(2,1)S(1)} %convolution_convert_fusion, bf16[2048,256]{1,0:T(8,128)(2,1)S(1)} %copy-done.4), kind=kOutput, calls=%fused_computation.8 | convolution fusion | flops 1080033280 | bytes 9961472 | tf_op jit(solution)/shard_map/dot_general | solution.py:39
  157.4 6.4 %copy.61 = bf16[2048,1024]{1,0:T(8,128)(2,1)} copy(bf16[2048,1024]{0,1:T(8,128)(2,1)} %fusion) | data formatting | bytes 8388608
  163.8 18.7 %gather_fusion = bf16[3072,1024]{1,0:T(8,128)(2,1)} fusion(bf16[2048,1024]{1,0:T(8,128)(2,1)} %copy.61, s32[3072]{0:T(1024)S(1)} %broadcast_clamp_fusion), kind=kCustom, calls=%fused_computation | custom fusion | bytes 12595200 | tf_op jit(solution)/shard_map/jit(_take)/gather | solution.py:48
  182.4 4.1 %broadcast_select_fusion = bf16[3072,1024]{1,0:T(8,128)(2,1)S(1)} fusion(bf16[3072,1024]{1,0:T(8,128)(2,1)} %gather_fusion, pred[3072]{0:T(1024)(128)(4,1)S(1)} %compare_and_fusion.1), kind=kLoop, calls=%fused_computation.36 | loop fusion | flops 3145728 | bytes 12585984 | tf_op jit(solution)/shard_map/jit(_take)/select_n | solution.py:48
  186.5 1.5 collective-permute-start
  188.1 4.1 %collective-permute-start.1 = (bf16[4,24,1024]{2,1,0:T(8,128)(2,1)S(1)}, bf16[4,24,1024]{2,1,0:T(8,128)(2,1)S(1)}, u32[]{:S(2)}, u32[]{:S(2)}) collective-permute-start(bf16[4,24,1024]{2,1,0:T(8,128)(2,1)S(1)} %bitcast.69), channel_id=1, source_target_pairs={{2,0},{4,2},{6,4},{8,6},{10,8},{12,10},{14,12},{16,14},{18,16},{20... | collective-permute-start | bytes 589832 | tf_op jit(solution)/shard_map/ppermute | solution.py:19
  192.2 0.7 broadcast_select_fusion.1
  193.0 2.9 collective-permute-done
  195.9 4.3 %fusion.12 = f32[128,16,1024]{2,1,0:T(8,128)} fusion(bf16[128,16,24]{2,1,0:T(8,128)(2,1)S(1)} %copy.47, bf16[4,24,1024]{2,1,0:T(8,128)(2,1)S(1)} %collective-permute-done, bf16[128,24,1024]{2,1,0:T(8,128)(2,1)S(1)} %broadcast_select_fusion.1), kind=kOutput, calls=%fused_computation.19 | convolution fusion | flops 103809024 | bytes 14974976 | tf_op jit(solution)/shard_map/aij,ajn->ain/dot_general | solution.py:60
  200.2 4.3 %fusion.15 = f32[128,16,1024]{2,1,0:T(8,128)} fusion(bf16[128,16,24]{2,1,0:T(8,128)(2,1)S(1)} %copy-done.5, bf16[4,24,1024]{2,1,0:T(8,128)(2,1)S(1)} %collective-permute-done, bf16[128,24,1024]{2,1,0:T(8,128)(2,1)S(1)} %broadcast_select_fusion.1), kind=kOutput, calls=%fused_computation.21 | convolution fusion | flops 103809024 | bytes 14974976 | tf_op jit(solution)/shard_map/aij,ajn->ain/dot_general | solution.py:60
  204.4 4.3 %fusion.18 = f32[128,16,1024]{2,1,0:T(8,128)} fusion(bf16[128,16,24]{2,1,0:T(8,128)(2,1)S(1)} %copy-done.6, bf16[4,24,1024]{2,1,0:T(8,128)(2,1)S(1)} %collective-permute-done, bf16[128,24,1024]{2,1,0:T(8,128)(2,1)S(1)} %broadcast_select_fusion.1), kind=kOutput, calls=%fused_computation.23 | convolution fusion | flops 103809024 | bytes 14974976 | tf_op jit(solution)/shard_map/aij,ajn->ain/dot_general | solution.py:60
  208.8 4.3 %fusion.25 = f32[128,16,1024]{2,1,0:T(8,128)} fusion(bf16[128,16,24]{2,1,0:T(8,128)(2,1)S(1)} %copy.49, bf16[128,24,1024]{2,1,0:T(8,128)(2,1)S(1)} %broadcast_select_fusion.1, bf16[4,24,1024]{2,1,0:T(8,128)(2,1)S(1)} %collective-permute-done), kind=kOutput, calls=%fused_computation.31 | convolution fusion | flops 103809024 | bytes 14974976 | tf_op jit(solution)/shard_map/aij,ajn->ain/dot_general | solution.py:60
  213.1 4.3 %fusion.6 = f32[128,16,1024]{2,1,0:T(8,128)} fusion(bf16[128,16,24]{2,1,0:T(8,128)(2,1)S(1)} %copy-done.7, bf16[4,24,1024]{2,1,0:T(8,128)(2,1)S(1)} %collective-permute-done.1, bf16[128,24,1024]{2,1,0:T(8,128)(2,1)S(1)} %broadcast_select_fusion.1), kind=kOutput, calls=%fused_computation.15 | convolution fusion | flops 103809024 | bytes 14974976 | tf_op jit(solution)/shard_map/aij,ajn->ain/dot_general | solution.py:60
  217.4 4.3 %fusion.9 = f32[128,16,1024]{2,1,0:T(8,128)} fusion(bf16[128,16,24]{2,1,0:T(8,128)(2,1)S(1)} %copy-done.8, bf16[4,24,1024]{2,1,0:T(8,128)(2,1)S(1)} %collective-permute-done.1, bf16[128,24,1024]{2,1,0:T(8,128)(2,1)S(1)} %broadcast_select_fusion.1), kind=kOutput, calls=%fused_computation.17 | convolution fusion | flops 103809024 | bytes 14974976 | tf_op jit(solution)/shard_map/aij,ajn->ain/dot_general | solution.py:60
  221.6 4.3 %fusion.3 = f32[128,16,1024]{2,1,0:T(8,128)} fusion(bf16[128,16,24]{2,1,0:T(8,128)(2,1)S(1)} %copy-done.9, bf16[4,24,1024]{2,1,0:T(8,128)(2,1)S(1)} %collective-permute-done.1, bf16[128,24,1024]{2,1,0:T(8,128)(2,1)S(1)} %broadcast_select_fusion.1), kind=kOutput, calls=%fused_computation.13 | convolution fusion | flops 103809024 | bytes 14974976 | tf_op jit(solution)/shard_map/aij,ajn->ain/dot_general | solution.py:60
  225.9 4.3 %fusion.20 = f32[128,16,1024]{2,1,0:T(8,128)} fusion(bf16[128,16,24]{2,1,0:T(8,128)(2,1)S(1)} %copy.59, bf16[4,24,1024]{2,1,0:T(8,128)(2,1)S(1)} %collective-permute-done.1, bf16[128,24,1024]{2,1,0:T(8,128)(2,1)S(1)} %broadcast_select_fusion.1), kind=kOutput, calls=%fused_computation.25 | convolution fusion | flops 103809024 | bytes 14974976 | tf_op jit(solution)/shard_map/aij,ajn->ain/dot_general | solution.py:60
  230.2 46.4 %fusion.37 = bf16[128,16,16]{2,1,0:T(8,128)(2,1)S(1)} fusion(f32[128,16,1024]{2,1,0:T(8,128)} %fusion.20, f32[128,16,1024]{2,1,0:T(8,128)} %fusion.3, f32[128,16,1024]{2,1,0:T(8,128)} %fusion.9, f32[128,16,1024]{2,1,0:T(8,128)} %fusion.6, f32[128,16,1024]{2,1,0:T(8,128)} %fusion.25, f32[128,16,1024]{2,1,0:T(8,128)} %fusion.12, ...), kind=kOutput, calls=%fused_computation.46 | convolution fusion | flops 316702720 | bytes 73576448 | tf_op jit(solution)/shard_map/ain,ajn->aij/dot_general | solution.py:70
  276.6 0.4 copy.60
  277.0 0.7 copy.63
  277.8 6.1 %reduce-scatter.4.cloned.1.call-done = bf16[64,256]{1,0:T(8,128)(2,1)} async-done(((bf16[128,256]{1,0:T(8,128)(2,1)}), bf16[64,256]{1,0:T(8,128)(2,1)}) %reduce-scatter.4.cloned.1.call-update) | async-done | bytes 32784
  283.9 0.9 copy.64
  284.7 0.7 copy.62
  (53 shorter events, 1.3 us)
Async XLA Ops:
  7.2 141.7 %copy-start = (f32[256,256]{1,0:T(8,128)S(1)}, f32[256,256]{1,0:T(8,128)}, u32[]{:S(2)}) copy-start(f32[256,256]{1,0:T(8,128)} %param.11) | copy-start | bytes 786436
  7.2 21.5 %all-gather.2.cloned.1.call-start = ((), (), s32[]{:S(2)}) async-start(), calls=%async_computation.1 | async-start | bytes 1572864 | tf_op jit(solution)/shard_map/all_gather | solution.py:35
  7.9 141.0 %all-reduce.2.cloned.1.call-start = ((), (), s32[]{:S(2)}) async-start(), calls=%async_computation.2 | async-start | bytes 2097152 | tf_op jit(solution)/shard_map/psum | solution.py:37
  13.7 14.8 %copy-start.11 = (f32[1024]{0:T(1024)S(1)}, f32[1024]{0:T(1024)}, u32[]{:S(2)}) copy-start(f32[1024]{0:T(1024)} %param.17) | copy-start | bytes 12292
  13.7 14.8 %copy-start.12 = (s32[1024]{0:T(1024)S(1)}, s32[1024]{0:T(1024)}, u32[]{:S(2)}) copy-start(s32[1024]{0:T(1024)} %param.16) | copy-start | bytes 12292
  13.7 14.8 %copy-start.10 = (s32[1,128]{1,0:T(1,128)S(1)}, s32[1,128]{1,0:T(1,128)}, u32[]{:S(2)}) copy-start(s32[1,128]{1,0:T(1,128)} %param.12) | copy-start | bytes 1540
  24.8 8.8 %copy-start.13 = (s32[128]{0:T(128)S(1)}, s32[128]{0:T(128)}, u32[]{:S(2)}) copy-start(s32[128]{0:T(128)} %param.13) | copy-start | bytes 1540
  28.7 123.2 %copy-start.4 = (bf16[2048,256]{1,0:T(8,128)(2,1)S(1)}, bf16[2048,256]{1,0:T(8,128)(2,1)}, u32[]{:S(2)}) copy-start(bf16[2048,256]{1,0:T(8,128)(2,1)} %all-gather.2.cloned.1.call-done) | copy-start | bytes 3145732
  33.6 250.3 %reduce-scatter.4.cloned.1.call-start = ((), (), s32[]{:S(2)}) async-start(), calls=%async_computation.3 | async-start | bytes 98304
  182.4 9.8 %copy-start.3 = (bf16[3072,1024]{1,0:T(8,128)(2,1)S(1)}, bf16[3072,1024]{1,0:T(8,128)(2,1)}, u32[]{:S(2)}) copy-start(bf16[3072,1024]{1,0:T(8,128)(2,1)} %gather_fusion) | copy-start | bytes 18874372
  186.5 9.3 %collective-permute-start = (bf16[4,24,1024]{2,1,0:T(8,128)(2,1)S(1)}, bf16[4,24,1024]{2,1,0:T(8,128)(2,1)S(1)}, u32[]{:S(2)}, u32[]{:S(2)}) collective-permute-start(bf16[4,24,1024]{2,1,0:T(8,128)(2,1)S(1)} %bitcast.70), channel_id=1, source_target_pairs={{0,2},{2,4},{4,6},{6,8},{8,10},{10,12},{12,14},{14,16},{16,18},{18... | collective-permute-start | bytes 589832 | tf_op jit(solution)/shard_map/ppermute | solution.py:18
  188.1 25.0 %collective-permute-start.1 = (bf16[4,24,1024]{2,1,0:T(8,128)(2,1)S(1)}, bf16[4,24,1024]{2,1,0:T(8,128)(2,1)S(1)}, u32[]{:S(2)}, u32[]{:S(2)}) collective-permute-start(bf16[4,24,1024]{2,1,0:T(8,128)(2,1)S(1)} %bitcast.69), channel_id=1, source_target_pairs={{2,0},{4,2},{6,4},{8,6},{10,8},{12,10},{14,12},{16,14},{18,16},{20... | collective-permute-start | bytes 589832 | tf_op jit(solution)/shard_map/ppermute | solution.py:19
  192.9 33.0 %copy-start.2 = (bf16[128,24,1024]{2,1,0:T(8,128)(2,1)}, bf16[128,24,1024]{2,1,0:T(8,128)(2,1)S(1)}, u32[]{:S(2)}) copy-start(bf16[128,24,1024]{2,1,0:T(8,128)(2,1)S(1)} %broadcast_select_fusion.1) | copy-start | bytes 18874372
  193.0 7.2 %copy-start.5 = (bf16[128,16,24]{2,1,0:T(8,128)(2,1)S(1)}, bf16[128,16,24]{2,1,0:T(8,128)(2,1)}, u32[]{:S(2)}) copy-start(bf16[128,16,24]{2,1,0:T(8,128)(2,1)} %copy.43) | copy-start | bytes 294916
  200.2 4.3 %copy-start.6 = (bf16[128,16,24]{2,1,0:T(8,128)(2,1)S(1)}, bf16[128,16,24]{2,1,0:T(8,128)(2,1)}, u32[]{:S(2)}) copy-start(bf16[128,16,24]{2,1,0:T(8,128)(2,1)} %copy.45) | copy-start | bytes 294916
  208.8 4.3 %copy-start.7 = (bf16[128,16,24]{2,1,0:T(8,128)(2,1)S(1)}, bf16[128,16,24]{2,1,0:T(8,128)(2,1)}, u32[]{:S(2)}) copy-start(bf16[128,16,24]{2,1,0:T(8,128)(2,1)} %copy.53) | copy-start | bytes 294916
  213.1 4.3 %copy-start.8 = (bf16[128,16,24]{2,1,0:T(8,128)(2,1)S(1)}, bf16[128,16,24]{2,1,0:T(8,128)(2,1)}, u32[]{:S(2)}) copy-start(bf16[128,16,24]{2,1,0:T(8,128)(2,1)} %copy.55) | copy-start | bytes 294916
  217.4 4.3 %copy-start.9 = (bf16[128,16,24]{2,1,0:T(8,128)(2,1)S(1)}, bf16[128,16,24]{2,1,0:T(8,128)(2,1)}, u32[]{:S(2)}) copy-start(bf16[128,16,24]{2,1,0:T(8,128)(2,1)} %copy.57) | copy-start | bytes 294916
  230.2 55.2 %copy-start.1 = (f32[256,256]{1,0:T(8,128)S(1)}, f32[256,256]{1,0:T(8,128)}, u32[]{:S(2)}) copy-start(f32[256,256]{1,0:T(8,128)} %param.11) | copy-start | bytes 786436
Sparse Core Ops, SparseCore 0:
  9.5 11.4 all-gather.1
  33.7 115.1 all-reduce.1
  277.9 5.9 reduce-scatter.3
where the time goes:
time: 293 us; the launch traced here: 292 us
  waiting for transfers between devices  125 us (43%)
  matrix products  94 us (32%)
  local copies, waits for them, and re-layouts  45.5 us (16%)
  between operations  14.1 us (5%)
  other arithmetic  7.78 us (3%)
  starting transfers between devices  5.79 us (2%)
    psum x1, waiting for transfers between devices, local(): inner_products = lax.psum(inner_products, 'row')  115 us
    dot_general x1, matrix products, local(): jnp.einsum('ain,ajn->aij', weighted, rounded, preferred_element_type=jnp....  46.4 us
    dot_general x8, matrix products, local(): jnp.einsum('aij,ajn->ain', blocks, neighbours, preferred_element_type=jnp...  34.3 us
    gather x1, local copies, waits for them, and re-layouts, local(): jnp.take(vectors, row_index.reshape(-1), axis=0, mode='fill', fill_value=0)  18.7 us
    unnamed x42, local copies, waits for them, and re-layouts  16.4 us
    select_n x9, local copies, waits for them, and re-layouts, local(): jnp.where(block_present[:, relative, None, None] > 0, blocks, jnp.zeros_l...  7.69 us
    unnamed x4, waiting for transfers between devices  6.78 us
  transfers between devices with their start and end apart: 5, of which 3 were waited for; matrix products, arithmetic and copies ran while one was open for 13% of the time, Pallas kernels for 0%

commit v1 on v0

--- a/solution.py
+++ b/solution.py
@@ -34,7 +34,8 @@
     cols_here = vectors_in.shape[1]
     whole_panel = lax.all_gather(panel, "col", axis=1, tiled=True)
     inner_products = panel_product(whole_panel, vectors_in)
-    inner_products = lax.psum(inner_products, "row")
+    shards = lax.all_gather(inner_products, "row")
+    inner_products = jnp.sum(shards, axis=0)
     mixing = jnp.dot(factor.T, inner_products, precision=lax.Precision.HIGHEST).astype(jnp.bfloat16)
     update = jnp.dot(whole_panel, mixing, preferred_element_type=jnp.float32)
     vectors = (vectors_in.astype(jnp.float32) - update).astype(jnp.bfloat16)

time: 293 us -> 369 us (1.26)
  waiting for transfers between devices: 125 us -> 199 us
  other arithmetic: 7.78 us -> 13.3 us
    all_gather x0 -> x1, waiting for transfers between devices: none -> 176 us  [local(): shards = lax.all_gather(inner_products, 'row')]
    psum x1 -> x0, waiting for transfers between devices: 115 us -> none  [local(): inner_products = lax.psum(inner_products, 'row')]
    all_gather x1, waiting for transfers between devices: 0.02 us -> 13.1 us  [local(): whole_panel = lax.all_gather(panel, 'col', axis=1, tiled=True)]
    reduce_sum x0 -> x1, other arithmetic: none -> 7.75 us  [local(): inner_products = jnp.sum(shards, axis=0)]
    unnamed x42 -> x44, local copies, waits for them, and re-layouts: 16.4 us -> 16.4 us
  transfers between devices with their start and end apart: 5 -> 5, of which waited for: 3 -> 4; matrix products, arithmetic and copies ran while one was open for 13% -> 9% of each run, Pallas kernels for 0% -> 0%
where the time goes in v1:
time: 369 us
  waiting for transfers between devices  199 us (54%)
  matrix products  93 us (25%)
  local copies, waits for them, and re-layouts  43.5 us (12%)
  between operations  14.1 us (4%)
  other arithmetic  13.3 us (4%)
  starting transfers between devices  5.79 us (2%)
    all_gather x1, waiting for transfers between devices, local(): shards = lax.all_gather(inner_products, 'row')  176 us
    dot_general x1, matrix products, local(): jnp.einsum('ain,ajn->aij', weighted, rounded, preferred_element_type=jnp....  46.4 us
    dot_general x8, matrix products, local(): jnp.einsum('aij,ajn->ain', blocks, neighbours, preferred_element_type=jnp...  34.3 us
    gather x1, local copies, waits for them, and re-layouts, local(): jnp.take(vectors, row_index.reshape(-1), axis=0, mode='fill', fill_value=0)  18.6 us
    unnamed x44, local copies, waits for them, and re-layouts  16.4 us
    all_gather x1, waiting for transfers between devices, local(): whole_panel = lax.all_gather(panel, 'col', axis=1, tiled=True)  13.1 us
    reduce_sum x1, other arithmetic, local(): inner_products = jnp.sum(shards, axis=0)  7.75 us
    select_n x9, local copies, waits for them, and re-layouts, local(): jnp.where(block_present[:, relative, None, None] > 0, blocks, jnp.zeros_l...  7.69 us
  transfers between devices with their start and end apart: 5, of which 4 were waited for; matrix products, arithmetic and copies ran while one was open for 9% of the time, Pallas kernels for 0%

profile of v1, /device:TPU:0, one launch (start us, length us, event | category | flops | bytes accessed | tf_op | source)
XLA Modules:
  0.0 368.7 jit_solution(13064107049780307365)
XLA Ops:
  7.2 0.7 all-gather.4.cloned.1.call-update
  8.0 13.1 %all-gather.4.cloned.1.call-done = bf16[2048,256]{1,0:T(8,128)(2,1)} async-done(((bf16[2048,128]{1,0:T(8,128)(2,1)}), bf16[2048,256]{1,0:T(8,128)(2,1)}) %all-gather.4.cloned.1.call-update) | async-done | bytes 1048592 | tf_op jit(solution)/shard_map/all_gather | solution.py:35
  21.1 4.8 %fusion.51 = f32[256,1024]{1,0:T(8,128)} fusion(bf16[2048,256]{1,0:T(8,128)(2,1)} %all-gather.4.cloned.1.call-done, bf16[2048,1024]{1,0:T(8,128)(2,1)} %param.9), kind=kOutput, calls=%fused_computation.88 | convolution fusion | flops 1073741824 | bytes 6291456 | tf_op jit(solution)/shard_map/dot_general | solution.py:25
  25.9 6.5 %copy.39 = bf16[2048,1024]{0,1:T(8,128)(2,1)} copy(bf16[2048,1024]{1,0:T(8,128)(2,1)} %param.9) | data formatting | bytes 8388608 | tf_op args[0]
  32.5 0.2 reduce-window.8
  33.2 0.1 copy.67
  33.4 0.1 copy.68
  33.6 0.4 copy.47
  34.0 0.1 copy.66
  34.1 0.1 copy.65
  34.3 1.2 copy.43
  35.5 1.2 copy.45
  36.7 0.4 copy.49
  37.1 0.1 copy.70
  37.2 0.1 copy.71
  37.4 1.2 copy.53
  38.6 1.2 copy.55
  39.8 0.1 copy.72
  39.9 0.1 copy.73
  40.1 1.2 copy.57
  41.3 0.4 copy.59
  41.7 0.1 copy.69
  41.8 0.4 copy.51
  42.6 175.6 %all-gather.6.cloned.1.call-done = f32[4096,1024]{1,0:T(8,128)} async-done(((f32[256,1024]{1,0:T(8,128)}), f32[4096,1024]{1,0:T(8,128)}) %all-gather.6.cloned.1.call-update) | async-done | bytes 16777232 | tf_op jit(solution)/shard_map/all_gather | solution.py:37
  218.2 7.7 %reduce_sum.9 = f32[256,1024]{1,0:T(8,128)S(1)} reduce(f32[16,256,1024]{2,1,0:T(8,128)} %bitcast.60, f32[]{:T(128)} %constant.10.clone.1), dimensions={0}, to_apply=%region_0.0 | reduce | flops 3932160 | bytes 17825796 | tf_op jit(solution)/shard_map/reduce_sum | solution.py:38
  226.0 1.8 convolution_convert_fusion
  227.8 5.8 %fusion = bf16[2048,1024]{0,1:T(8,128)(2,1)} fusion(bf16[2048,1024]{0,1:T(8,128)(2,1)} %copy.39, bf16[1024,256]{1,0:T(8,128)(2,1)S(1)} %convolution_convert_fusion, bf16[2048,256]{1,0:T(8,128)(2,1)} %all-gather.4.cloned.1.call-done), kind=kOutput, calls=%fused_computation.8 | convolution fusion | flops 1080033280 | bytes 9961472 | tf_op jit(solution)/shard_map/dot_general | solution.py:40
  233.5 6.4 %copy.61 = bf16[2048,1024]{1,0:T(8,128)(2,1)} copy(bf16[2048,1024]{0,1:T(8,128)(2,1)} %fusion) | data formatting | bytes 8388608
  239.9 18.6 %gather_fusion = bf16[3072,1024]{1,0:T(8,128)(2,1)} fusion(bf16[2048,1024]{1,0:T(8,128)(2,1)} %copy.61, s32[3072]{0:T(1024)S(1)} %broadcast_clamp_fusion), kind=kCustom, calls=%fused_computation | custom fusion | bytes 12595200 | tf_op jit(solution)/shard_map/jit(_take)/gather | solution.py:49
  258.5 4.1 %broadcast_select_fusion = bf16[3072,1024]{1,0:T(8,128)(2,1)S(1)} fusion(bf16[3072,1024]{1,0:T(8,128)(2,1)} %gather_fusion, pred[3072]{0:T(1024)(128)(4,1)S(1)} %compare_and_fusion.1), kind=kLoop, calls=%fused_computation.36 | loop fusion | flops 3145728 | bytes 12585984 | tf_op jit(solution)/shard_map/jit(_take)/select_n | solution.py:49
  262.6 1.5 collective-permute-start
  264.1 4.2 %collective-permute-start.1 = (bf16[4,24,1024]{2,1,0:T(8,128)(2,1)S(1)}, bf16[4,24,1024]{2,1,0:T(8,128)(2,1)S(1)}, u32[]{:S(2)}, u32[]{:S(2)}) collective-permute-start(bf16[4,24,1024]{2,1,0:T(8,128)(2,1)S(1)} %bitcast.71), channel_id=1, source_target_pairs={{2,0},{4,2},{6,4},{8,6},{10,8},{12,10},{14,12},{16,14},{18,16},{20... | collective-permute-start | bytes 589832 | tf_op jit(solution)/shard_map/ppermute | solution.py:19
  268.3 0.7 broadcast_select_fusion.1
  269.0 3.3 collective-permute-done
  272.3 4.3 %fusion.12 = f32[128,16,1024]{2,1,0:T(8,128)} fusion(bf16[128,16,24]{2,1,0:T(8,128)(2,1)S(1)} %copy.47, bf16[4,24,1024]{2,1,0:T(8,128)(2,1)S(1)} %collective-permute-done, bf16[128,24,1024]{2,1,0:T(8,128)(2,1)S(1)} %broadcast_select_fusion.1), kind=kOutput, calls=%fused_computation.19 | convolution fusion | flops 103809024 | bytes 14974976 | tf_op jit(solution)/shard_map/aij,ajn->ain/dot_general | solution.py:61
  276.6 4.2 %fusion.15 = f32[128,16,1024]{2,1,0:T(8,128)} fusion(bf16[128,16,24]{2,1,0:T(8,128)(2,1)S(1)} %copy-done.5, bf16[4,24,1024]{2,1,0:T(8,128)(2,1)S(1)} %collective-permute-done, bf16[128,24,1024]{2,1,0:T(8,128)(2,1)S(1)} %broadcast_select_fusion.1), kind=kOutput, calls=%fused_computation.21 | convolution fusion | flops 103809024 | bytes 14974976 | tf_op jit(solution)/shard_map/aij,ajn->ain/dot_general | solution.py:61
  280.8 4.3 %fusion.18 = f32[128,16,1024]{2,1,0:T(8,128)} fusion(bf16[128,16,24]{2,1,0:T(8,128)(2,1)S(1)} %copy-done.6, bf16[4,24,1024]{2,1,0:T(8,128)(2,1)S(1)} %collective-permute-done, bf16[128,24,1024]{2,1,0:T(8,128)(2,1)S(1)} %broadcast_select_fusion.1), kind=kOutput, calls=%fused_computation.23 | convolution fusion | flops 103809024 | bytes 14974976 | tf_op jit(solution)/shard_map/aij,ajn->ain/dot_general | solution.py:61
  285.1 4.3 %fusion.25 = f32[128,16,1024]{2,1,0:T(8,128)} fusion(bf16[128,16,24]{2,1,0:T(8,128)(2,1)S(1)} %copy.49, bf16[128,24,1024]{2,1,0:T(8,128)(2,1)S(1)} %broadcast_select_fusion.1, bf16[4,24,1024]{2,1,0:T(8,128)(2,1)S(1)} %collective-permute-done), kind=kOutput, calls=%fused_computation.31 | convolution fusion | flops 103809024 | bytes 14974976 | tf_op jit(solution)/shard_map/aij,ajn->ain/dot_general | solution.py:61
  289.5 4.3 %fusion.6 = f32[128,16,1024]{2,1,0:T(8,128)} fusion(bf16[128,16,24]{2,1,0:T(8,128)(2,1)S(1)} %copy-done.7, bf16[4,24,1024]{2,1,0:T(8,128)(2,1)S(1)} %collective-permute-done.1, bf16[128,24,1024]{2,1,0:T(8,128)(2,1)S(1)} %broadcast_select_fusion.1), kind=kOutput, calls=%fused_computation.15 | convolution fusion | flops 103809024 | bytes 14974976 | tf_op jit(solution)/shard_map/aij,ajn->ain/dot_general | solution.py:61
  293.8 4.3 %fusion.9 = f32[128,16,1024]{2,1,0:T(8,128)} fusion(bf16[128,16,24]{2,1,0:T(8,128)(2,1)S(1)} %copy-done.8, bf16[4,24,1024]{2,1,0:T(8,128)(2,1)S(1)} %collective-permute-done.1, bf16[128,24,1024]{2,1,0:T(8,128)(2,1)S(1)} %broadcast_select_fusion.1), kind=kOutput, calls=%fused_computation.17 | convolution fusion | flops 103809024 | bytes 14974976 | tf_op jit(solution)/shard_map/aij,ajn->ain/dot_general | solution.py:61
  298.0 4.3 %fusion.3 = f32[128,16,1024]{2,1,0:T(8,128)} fusion(bf16[128,16,24]{2,1,0:T(8,128)(2,1)S(1)} %copy-done.9, bf16[4,24,1024]{2,1,0:T(8,128)(2,1)S(1)} %collective-permute-done.1, bf16[128,24,1024]{2,1,0:T(8,128)(2,1)S(1)} %broadcast_select_fusion.1), kind=kOutput, calls=%fused_computation.13 | convolution fusion | flops 103809024 | bytes 14974976 | tf_op jit(solution)/shard_map/aij,ajn->ain/dot_general | solution.py:61
  302.3 4.3 %fusion.20 = f32[128,16,1024]{2,1,0:T(8,128)} fusion(bf16[128,16,24]{2,1,0:T(8,128)(2,1)S(1)} %copy.59, bf16[4,24,1024]{2,1,0:T(8,128)(2,1)S(1)} %collective-permute-done.1, bf16[128,24,1024]{2,1,0:T(8,128)(2,1)S(1)} %broadcast_select_fusion.1), kind=kOutput, calls=%fused_computation.25 | convolution fusion | flops 103809024 | bytes 14974976 | tf_op jit(solution)/shard_map/aij,ajn->ain/dot_general | solution.py:61
  306.6 46.4 %fusion.37 = bf16[128,16,16]{2,1,0:T(8,128)(2,1)S(1)} fusion(f32[128,16,1024]{2,1,0:T(8,128)} %fusion.20, f32[128,16,1024]{2,1,0:T(8,128)} %fusion.3, f32[128,16,1024]{2,1,0:T(8,128)} %fusion.9, f32[128,16,1024]{2,1,0:T(8,128)} %fusion.6, f32[128,16,1024]{2,1,0:T(8,128)} %fusion.25, f32[128,16,1024]{2,1,0:T(8,128)} %fusion.12, ...), kind=kOutput, calls=%fused_computation.46 | convolution fusion | flops 316702720 | bytes 73576448 | tf_op jit(solution)/shard_map/ain,ajn->aij/dot_general | solution.py:71
  353.0 0.4 copy.60
  353.4 0.7 copy.63
  354.2 6.3 %reduce-scatter.4.cloned.1.call-done = bf16[64,256]{1,0:T(8,128)(2,1)} async-done(((bf16[128,256]{1,0:T(8,128)(2,1)}), bf16[64,256]{1,0:T(8,128)(2,1)}) %reduce-scatter.4.cloned.1.call-update) | async-done | bytes 32784
  360.5 0.9 copy.64
  361.4 0.7 copy.62
  (56 shorter events, 1.2 us)
Async XLA Ops:
  7.2 218.8 %copy-start = (f32[256,256]{1,0:T(8,128)S(1)}, f32[256,256]{1,0:T(8,128)}, u32[]{:S(2)}) copy-start(f32[256,256]{1,0:T(8,128)} %param.11) | copy-start | bytes 786436
  7.2 13.9 %all-gather.4.cloned.1.call-start = ((), (), s32[]{:S(2)}) async-start(), calls=%async_computation.1 | async-start | bytes 1572864 | tf_op jit(solution)/shard_map/all_gather | solution.py:35
  7.9 210.3 %all-gather.6.cloned.1.call-start = ((), (), s32[]{:S(2)}) async-start(), calls=%async_computation.2 | async-start | bytes 17825792 | tf_op jit(solution)/shard_map/all_gather | solution.py:37
  25.8 6.6 %copy-start.10 = (s32[1,128]{1,0:T(1,128)S(1)}, s32[1,128]{1,0:T(1,128)}, u32[]{:S(2)}) copy-start(s32[1,128]{1,0:T(1,128)} %param.12) | copy-start | bytes 1540
  25.8 7.3 %copy-start.4 = (bf16[128,9,384]{2,0,1:T(8,128)(2,1)S(1)}, bf16[128,9,384]{2,0,1:T(8,128)(2,1)}, u32[]{:S(2)}) copy-start(bf16[128,9,384]{2,0,1:T(8,128)(2,1)} %param.14) | copy-start | bytes 2654212
  25.8 7.7 %copy-start.13 = (s32[128,9]{0,1:T(8,128)S(1)}, s32[128,9]{0,1:T(8,128)}, u32[]{:S(2)}) copy-start(s32[128,9]{0,1:T(8,128)} %param.15) | copy-start | bytes 13828
  25.8 334.7 %reduce-scatter.4.cloned.1.call-start = ((), (), s32[]{:S(2)}) async-start(), calls=%async_computation.3 | async-start | bytes 98304
  32.4 9.9 %copy-start.11 = (f32[1024]{0:T(1024)S(1)}, f32[1024]{0:T(1024)}, u32[]{:S(2)}) copy-start(f32[1024]{0:T(1024)} %param.17) | copy-start | bytes 12292
  32.4 9.9 %copy-start.12 = (s32[1024]{0:T(1024)S(1)}, s32[1024]{0:T(1024)}, u32[]{:S(2)}) copy-start(s32[1024]{0:T(1024)} %param.16) | copy-start | bytes 12292
  32.4 10.1 %copy-start.14 = (s32[128]{0:T(128)S(1)}, s32[128]{0:T(128)}, u32[]{:S(2)}) copy-start(s32[128]{0:T(128)} %param.13) | copy-start | bytes 1540
  258.5 9.8 %copy-start.3 = (bf16[3072,1024]{1,0:T(8,128)(2,1)S(1)}, bf16[3072,1024]{1,0:T(8,128)(2,1)}, u32[]{:S(2)}) copy-start(bf16[3072,1024]{1,0:T(8,128)(2,1)} %gather_fusion) | copy-start | bytes 18874372
  262.6 9.7 %collective-permute-start = (bf16[4,24,1024]{2,1,0:T(8,128)(2,1)S(1)}, bf16[4,24,1024]{2,1,0:T(8,128)(2,1)S(1)}, u32[]{:S(2)}, u32[]{:S(2)}) collective-permute-start(bf16[4,24,1024]{2,1,0:T(8,128)(2,1)S(1)} %bitcast.72), channel_id=1, source_target_pairs={{0,2},{2,4},{4,6},{6,8},{8,10},{10,12},{12,14},{14,16},{16,18},{18... | collective-permute-start | bytes 589832 | tf_op jit(solution)/shard_map/ppermute | solution.py:18
  264.1 25.4 %collective-permute-start.1 = (bf16[4,24,1024]{2,1,0:T(8,128)(2,1)S(1)}, bf16[4,24,1024]{2,1,0:T(8,128)(2,1)S(1)}, u32[]{:S(2)}, u32[]{:S(2)}) collective-permute-start(bf16[4,24,1024]{2,1,0:T(8,128)(2,1)S(1)} %bitcast.71), channel_id=1, source_target_pairs={{2,0},{4,2},{6,4},{8,6},{10,8},{12,10},{14,12},{16,14},{18,16},{20... | collective-permute-start | bytes 589832 | tf_op jit(solution)/shard_map/ppermute | solution.py:19
  269.0 33.3 %copy-start.2 = (bf16[128,24,1024]{2,1,0:T(8,128)(2,1)}, bf16[128,24,1024]{2,1,0:T(8,128)(2,1)S(1)}, u32[]{:S(2)}) copy-start(bf16[128,24,1024]{2,1,0:T(8,128)(2,1)S(1)} %broadcast_select_fusion.1) | copy-start | bytes 18874372
  269.0 7.6 %copy-start.5 = (bf16[128,16,24]{2,1,0:T(8,128)(2,1)S(1)}, bf16[128,16,24]{2,1,0:T(8,128)(2,1)}, u32[]{:S(2)}) copy-start(bf16[128,16,24]{2,1,0:T(8,128)(2,1)} %copy.43) | copy-start | bytes 294916
  276.6 4.2 %copy-start.6 = (bf16[128,16,24]{2,1,0:T(8,128)(2,1)S(1)}, bf16[128,16,24]{2,1,0:T(8,128)(2,1)}, u32[]{:S(2)}) copy-start(bf16[128,16,24]{2,1,0:T(8,128)(2,1)} %copy.45) | copy-start | bytes 294916
  285.1 4.3 %copy-start.7 = (bf16[128,16,24]{2,1,0:T(8,128)(2,1)S(1)}, bf16[128,16,24]{2,1,0:T(8,128)(2,1)}, u32[]{:S(2)}) copy-start(bf16[128,16,24]{2,1,0:T(8,128)(2,1)} %copy.53) | copy-start | bytes 294916
  289.5 4.3 %copy-start.8 = (bf16[128,16,24]{2,1,0:T(8,128)(2,1)S(1)}, bf16[128,16,24]{2,1,0:T(8,128)(2,1)}, u32[]{:S(2)}) copy-start(bf16[128,16,24]{2,1,0:T(8,128)(2,1)} %copy.55) | copy-start | bytes 294916
  293.8 4.3 %copy-start.9 = (bf16[128,16,24]{2,1,0:T(8,128)(2,1)S(1)}, bf16[128,16,24]{2,1,0:T(8,128)(2,1)}, u32[]{:S(2)}) copy-start(bf16[128,16,24]{2,1,0:T(8,128)(2,1)} %copy.57) | copy-start | bytes 294916
  306.6 55.5 %copy-start.1 = (f32[256,256]{1,0:T(8,128)S(1)}, f32[256,256]{1,0:T(8,128)}, u32[]{:S(2)}) copy-start(f32[256,256]{1,0:T(8,128)} %param.11) | copy-start | bytes 786436
Sparse Core Ops, SparseCore 0:
  9.5 11.4 all-gather.3
  26.0 192.1 all-gather.5
  354.3 6.1 reduce-scatter.3
